TPU v7x, 32 devices: a whole 2x2x4 slice. The times are simulated.
32 devices in a mesh: tbl: 8 (over z, y), pair: 4 (over x, core).
Axes of the slice: x: 2, y: 2, z: 4, core: 2. Of those that a mesh axis runs over, the one named last changes fastest.
Arguments:
- codes: bfloat16 [112, 64, 16384], P('tbl', None, 'pair'), may hold values from -127 to 127
- scales: float32 [112, 16384], P('tbl', 'pair'), may hold values from 0.002 to 0.02
- shard_slot: int32 [8, 14], replicated, may hold values from -1 to 53, as said below
- weight_first: bfloat16 [351, 1024], replicated, may hold values from -0.3125 to 0.3125
- bias_first: float32 [1024], replicated, may hold values from -3 to 3
- weight_second: bfloat16 [1024, 1024], replicated, may hold values from -0.1875 to 0.1875
- bias_second: float32 [1024], replicated, may hold values from -3 to 3
- weight_third: bfloat16 [1024, 512], replicated, may hold values from -0.1875 to 0.1875
- bias_third: float32 [512], replicated, may hold values from -3 to 3
- weight_fourth: bfloat16 [512, 256], replicated, may hold values from -0.25 to 0.25
- bias_fourth: float32 [256], replicated, may hold values from -3 to 3
- weight_out: bfloat16 [256], replicated, may hold values from -0.375 to 0.375
- bias_out: float32 [1], replicated, may hold values from -3 to 3
Outputs:
- logits: float32 [4, 4096], P(None, 'tbl')
Inputs may be any that keep to these rules, and one draw needn't show every extreme that they name: `shard_slot`: each shard 0 to 53 stands in exactly one slot; all other slots hold -1. For k below half of the tbl size, row k holds its shards in its first slots and the row half the tbl size further holds its shards in its last slots, and the two rows hold 14 shards or fewer together. Some row holds 14 shards.
All inputs are finite; a program needn't handle non-finite values.
Results may differ from a plain program's by a relative error of at most 0.03.
Values may be sent and summed in bfloat16 or wider, within the bound.
No kernel may reach another device: no remote copies, remote signals or barrier semaphores. Data moves between devices by JAX's collectives and lax.ppermute only.
A program may use at most 128 MiB of HBM per device.

v0:
```python
import jax
import jax.numpy as jnp
import numpy as np
from jax import lax
from jax.sharding import PartitionSpec as P

TABLES = 27


def pair_columns(tables):
    first, second = np.triu_indices(tables, 1)
    return (first * tables + second).astype(np.int32)


def shard_positions(slot_table, shard_total):
    flat = slot_table.reshape(-1)
    matches = flat[None, :] == jnp.arange(shard_total, dtype=jnp.int32)[:, None]
    places = jnp.arange(flat.shape[0], dtype=jnp.int32)[None, :]
    return jnp.sum(jnp.where(matches, places, 0), axis=1)


def dense_layer(inputs, weight, bias):
    product = jnp.dot(
        inputs.astype(jnp.float32), weight.astype(jnp.float32), precision=lax.Precision.HIGHEST
    )
    return jax.nn.relu(product + bias).astype(jnp.bfloat16)


def score_samples(picked_codes, picked_scales, layers):
    table_count = picked_codes.shape[0] // 2
    column_count = picked_codes.shape[1]
    count = picked_codes.shape[2]
    halves = picked_codes.reshape(table_count, 2, column_count, count)
    half_scales = picked_scales.reshape(table_count, 2, count)
    gram = jnp.zeros((count, table_count, table_count), jnp.float32)
    for part_index in range(2):
        block_codes = halves[:, part_index].astype(jnp.float32)
        products = jnp.einsum(
            "icb,jcb->bij", block_codes, block_codes, precision=lax.Precision.HIGHEST
        )
        factor = half_scales[:, part_index]
        outer = jnp.transpose(factor)[:, :, None] * jnp.transpose(factor)[:, None, :]
        gram = gram + products * outer
    flat = gram.reshape(count, table_count * table_count)
    hidden = flat[:, pair_columns(table_count)].astype(jnp.bfloat16)
    for weight, bias in layers[:-1]:
        hidden = dense_layer(hidden, weight, bias)
    weight_last, bias_last = layers[-1]
    final = jnp.dot(
        hidden.astype(jnp.float32), weight_last.astype(jnp.float32), precision=lax.Precision.HIGHEST
    )
    return final + bias_last[0]


def per_device(
    codes,
    scales,
    shard_slot,
    weight_first,
    bias_first,
    weight_second,
    bias_second,
    weight_third,
    bias_third,
    weight_fourth,
    bias_fourth,
    weight_out,
    bias_out,
):
    layers = (
        (weight_first, bias_first),
        (weight_second, bias_second),
        (weight_third, bias_third),
        (weight_fourth, bias_fourth),
        (weight_out, bias_out),
    )
    slot_count = codes.shape[0]
    column_count = codes.shape[1]
    tbl_count = lax.axis_size("tbl")
    batch_local = codes.shape[2] // tbl_count
    shard_total = 2 * TABLES

    def make_scorer(positions):

        def scorer(received):
            got_codes, got_scales = received
            picked_codes = jnp.take(got_codes[:, :, 0, :], positions, axis=0)
            picked_scales = jnp.take(got_scales[:, 0, 0, :], positions, axis=0)
            return score_samples(picked_codes, picked_scales, layers)

        return scorer

    packed_codes = codes.reshape(slot_count, column_count, tbl_count, batch_local)
    packed_scales = scales.reshape(slot_count, 1, tbl_count, batch_local)
    scorer = make_scorer(shard_positions(shard_slot, shard_total))
    logits = scorer(
        (
            lax.all_to_all(packed_codes, "tbl", split_axis=2, concat_axis=0, tiled=True),
            lax.all_to_all(
                packed_scales.astype(jnp.bfloat16), "tbl", split_axis=2, concat_axis=0, tiled=True
            ).astype(packed_scales.dtype),
        )
    )
    return lax.all_gather(logits[None, :], "pair", axis=0, tiled=True)


def solution(mesh):
    return jax.shard_map(
        per_device,
        mesh=mesh,
        in_specs=(
            P("tbl", None, "pair"),
            P("tbl", "pair"),
            P(),
            P(),
            P(),
            P(),
            P(),
            P(),
            P(),
            P(),
            P(),
            P(),
            P(),
        ),
        out_specs=P(None, "tbl"),
        check_vma=False,
    )
```

profile of v0, /device:TPU:0, one launch (start us, length us, event | category | flops | bytes accessed | tf_op | source)
XLA Modules:
  0.0 243.0 jit_solution(14735998043598674516)
XLA Ops:
  0.0 0.0 copy-start
  0.0 1.1 convert_element_type.56
  1.2 0.7 copy.51
  1.9 7.3 %all-to-all-start.1 = ((bf16[14,1,8,512]{3,0,1,2:T(8,128)(2,1)}), bf16[14,1,8,512]{3,0,1,2:T(8,128)(2,1)S(1)}, u32[]{:S(2)}, u32[]{:S(2)}) async-start(bf16[14,1,8,512]{3,0,1,2:T(8,128)(2,1)} %copy.51), calls=%async_computation.1 | async-start | bytes 262144 | tf_op jit(solution)/shard_map/all_to_all | solution.py:99
  9.2 7.2 %copy.60 = bf16[14,8,8,8,512]{4,3,1,0,2:T(8,128)(2,1)} copy(bf16[14,8,8,8,512]{4,3,2,1,0:T(8,128)(2,1)} %bitcast.62) | data formatting | bytes 14680064 | tf_op jit(solution)/shard_map/reshape | solution.py:93
  16.4 0.1 all-to-all-done.1
  16.5 0.0 copy-start.2
  16.5 0.0 copy-start.10
  16.5 0.0 copy-start.3
  16.5 6.0 %all-to-all-start = ((bf16[14,64,8,512]{3,1,0,2:T(8,128)(2,1)}), bf16[14,64,8,512]{3,1,0,2:T(8,128)(2,1)}, u32[]{:S(2)}, u32[]{:S(2)}) async-start(bf16[14,64,8,512]{3,1,0,2:T(8,128)(2,1)} %bitcast.60), calls=%async_computation | async-start | bytes 14680064 | tf_op jit(solution)/shard_map/all_to_all | solution.py:98
  22.6 0.0 copy-done.2
  22.6 0.1 eq.15
  22.6 0.1 select_reduce_fusion
  22.8 0.1 reduce_sum.14
  22.9 0.1 copy.47
  23.0 0.0 copy-done.10
  23.7 0.0 copy-done.3
  23.8 0.6 gather_fusion.1
  24.4 0.1 gather.18
  24.5 0.2 copy.52
  24.8 157.9 %all-to-all-done = bf16[14,64,8,512]{3,1,0,2:T(8,128)(2,1)} async-done(((bf16[14,64,8,512]{3,1,0,2:T(8,128)(2,1)}), bf16[14,64,8,512]{3,1,0,2:T(8,128)(2,1)}, u32[]{:S(2)}, u32[]{:S(2)}) %all-to-all-start) | async-done | bytes 7340064 | tf_op jit(solution)/shard_map/all_to_all | solution.py:98
  182.7 5.7 %gather_fusion = bf16[54,64,512]{2,1,0:T(8,128)(2,1)} fusion(bf16[112,64,512]{2,1,0:T(8,128)(2,1)} %bitcast.2, s32[1024]{0:T(1024)S(1)} %pad_clamp_fusion.1), kind=kCustom, calls=%fused_computation | custom fusion | bytes 7078104 | tf_op jit(solution)/shard_map/jit(_take)/gather | solution.py:87
  188.4 13.0 %copy.49 = bf16[27,2,64,512]{2,0,3,1:T(8,128)(2,1)} copy(bf16[27,2,64,512]{3,2,1,0:T(8,128)(2,1)} %bitcast.61) | data formatting | bytes 7077888 | tf_op jit(solution)/shard_map/jit(_take)/gather | solution.py:87
  201.5 7.4 %broadcast_select_fusion = bf16[27,2,64,512]{2,0,3,1:T(8,128)(2,1)} fusion(bf16[27,2,64,512]{2,0,3,1:T(8,128)(2,1)} %copy.49, pred[27,2]{0,1:T(4,128)(4,1)S(1)} %copy.47), kind=kLoop, calls=%fused_computation.4 | loop fusion | flops 1769472 | bytes 7077942 | tf_op jit(solution)/shard_map/jit(_take)/select_n | solution.py:87
  208.9 0.0 copy-start.1
  208.9 5.9 %fusion = f32[512,27,27]{2,1,0:T(8,128)S(1)} fusion(bf16[27,2,64,512]{2,0,3,1:T(8,128)(2,1)} %broadcast_select_fusion), kind=kOutput, calls=%fused_computation.7 | convolution fusion | flops 47775744 | bytes 5687296 | tf_op jit(solution)/shard_map/icb,jcb->bij/dot_general | solution.py:38
  214.7 0.0 copy-done.1
  214.7 6.7 %multiply_add_fusion = bf16[512,27,27]{2,1,0:T(8,128)(2,1)} fusion(f32[512,27,27]{2,1,0:T(8,128)S(1)} %fusion, f32[512,27]{1,0:T(8,128)S(1)} %get-tuple-element.6, f32[512,27]{1,0:T(8,128)S(1)} %get-tuple-element.5, bf16[27,2,64,512]{2,0,3,1:T(8,128)(2,1)S(1)} %copy-done.1), kind=kOutput, calls=%fused_computation.3 | convolution fusion | flops 50015232 | bytes 14377984 | tf_op jit(solution)/shard_map/icb,jcb->bij/dot_general | solution.py:38
  221.5 0.0 copy-start.6
  221.5 0.0 copy-start.7
  221.5 7.7 %reshape.100 = bf16[512,729]{1,0:T(8,128)(2,1)} reshape(bf16[512,27,27]{2,1,0:T(8,128)(2,1)} %multiply_add_fusion) | data formatting | bytes 1492992 | tf_op jit(solution)/shard_map/reshape | solution.py:44
  229.2 1.4 copy.54
  230.6 0.0 copy-start.8
  230.6 2.0 gather_fusion.2
  232.7 0.0 copy-done.6
  232.7 0.0 copy-start.4
  232.7 0.0 copy-start.5
  232.7 0.0 copy-start.9
  232.7 1.9 maximum_convert_fusion.1
  234.7 0.0 copy-done
  234.7 0.0 copy-done.7
  234.7 1.3 maximum_convert_fusion
  236.0 0.0 copy-done.8
  236.0 0.0 copy-done.4
  236.0 0.7 fusion.3
  236.7 0.0 copy-done.5
  236.7 0.0 copy-done.9
  236.7 0.3 fusion.5
  237.0 0.2 fusion.8
  237.2 5.2 %all-gather.1 = f32[4,1,512]{2,1,0:T(1,128)S(1)} all-gather(f32[1,1,512]{2,1,0:T(1,128)S(1)} %bitcast.66), channel_id=2, replica_groups=mesh['tbl'=8,'pair'=4] {'pair'}, dimensions={0}, use_global_device_ids=true | all-gather | bytes 10240 | tf_op jit(solution)/shard_map/all_gather | solution.py:104
  242.4 0.6 copy.61
  (12 shorter events, 0.2 us)
Async XLA Ops:
  0.0 234.7 %copy-start = (bf16[1024,1024]{1,0:T(8,128)(2,1)S(1)}, bf16[1024,1024]{1,0:T(8,128)(2,1)}, u32[]{:S(2)}) copy-start(bf16[1024,1024]{1,0:T(8,128)(2,1)} %param.20) | copy-start | bytes 6291460
  1.9 14.7 %all-to-all-start.1 = ((bf16[14,1,8,512]{3,0,1,2:T(8,128)(2,1)}), bf16[14,1,8,512]{3,0,1,2:T(8,128)(2,1)S(1)}, u32[]{:S(2)}, u32[]{:S(2)}) async-start(bf16[14,1,8,512]{3,0,1,2:T(8,128)(2,1)} %copy.51), calls=%async_computation.1 | async-start | bytes 262144 | tf_op jit(solution)/shard_map/all_to_all | solution.py:99
  16.5 6.0 %copy-start.2 = (s32[8,14]{1,0:T(8,128)S(1)}, s32[8,14]{1,0:T(8,128)}, u32[]{:S(2)}) copy-start(s32[8,14]{1,0:T(8,128)} %param.17) | copy-start | bytes 1348
  16.5 6.5 %copy-start.10 = (bf16[256]{0:T(256)(128)(2,1)S(1)}, bf16[256]{0:T(256)(128)(2,1)}, u32[]{:S(2)}) copy-start(bf16[256]{0:T(256)(128)(2,1)} %param.26) | copy-start | bytes 1540
  16.5 7.1 %copy-start.3 = (s32[351]{0:T(512)S(1)}, s32[351]{0:T(512)}, u32[]{:S(2)}) copy-start(s32[351]{0:T(512)} %constant.49) | copy-start | bytes 4216
  16.5 166.2 %all-to-all-start = ((bf16[14,64,8,512]{3,1,0,2:T(8,128)(2,1)}), bf16[14,64,8,512]{3,1,0,2:T(8,128)(2,1)}, u32[]{:S(2)}, u32[]{:S(2)}) async-start(bf16[14,64,8,512]{3,1,0,2:T(8,128)(2,1)} %bitcast.60), calls=%async_computation | async-start | bytes 14680064 | tf_op jit(solution)/shard_map/all_to_all | solution.py:98
  208.9 5.9 %copy-start.1 = (bf16[27,2,64,512]{2,0,3,1:T(8,128)(2,1)S(1)}, bf16[27,2,64,512]{2,0,3,1:T(8,128)(2,1)}, u32[]{:S(2)}) copy-start(bf16[27,2,64,512]{2,0,3,1:T(8,128)(2,1)} %broadcast_select_fusion) | copy-start | bytes 10616836
  221.5 11.2 %copy-start.6 = (f32[1024]{0:T(1024)S(1)}, f32[1024]{0:T(1024)}, u32[]{:S(2)}) copy-start(f32[1024]{0:T(1024)} %param.19) | copy-start | bytes 12292
  221.5 13.2 %copy-start.7 = (f32[1024]{0:T(1024)S(1)}, f32[1024]{0:T(1024)}, u32[]{:S(2)}) copy-start(f32[1024]{0:T(1024)} %param.21) | copy-start | bytes 12292
  230.6 5.4 %copy-start.8 = (f32[512]{0:T(512)S(1)}, f32[512]{0:T(512)}, u32[]{:S(2)}) copy-start(f32[512]{0:T(512)} %param.23) | copy-start | bytes 6148
  232.7 3.3 %copy-start.4 = (bf16[1024,512]{1,0:T(8,128)(2,1)S(1)}, bf16[1024,512]{1,0:T(8,128)(2,1)}, u32[]{:S(2)}) copy-start(bf16[1024,512]{1,0:T(8,128)(2,1)} %param.22) | copy-start | bytes 3145732
  232.7 4.0 %copy-start.5 = (bf16[512,256]{1,0:T(8,128)(2,1)S(1)}, bf16[512,256]{1,0:T(8,128)(2,1)}, u32[]{:S(2)}) copy-start(bf16[512,256]{1,0:T(8,128)(2,1)} %param.24) | copy-start | bytes 786436
  232.7 4.0 %copy-start.9 = (f32[256]{0:T(256)S(1)}, f32[256]{0:T(256)}, u32[]{:S(2)}) copy-start(f32[256]{0:T(256)} %param.25) | copy-start | bytes 3076
where the time goes:
time: 244 us; the launch traced here: 243 us
  waiting for transfers between devices  158 us (65%)
  local copies, waits for them, and re-layouts  39.8 us (16%)
  matrix products  17 us (7%)
  starting transfers between devices  13.3 us (5%)
  other arithmetic  8.71 us (4%)
  blocking collectives  5.2 us (2%)
    all_to_all x1, waiting for transfers between devices, per_device(): lax.all_to_all(packed_codes, 'tbl', split_axis=2, concat_axis=0, tiled=True)  158 us
    gather x2, local copies, waits for them, and re-layouts, scorer(): picked_codes = jnp.take(got_codes[:, :, 0, :], positions, axis=0)  18.8 us
    dot_general x2, matrix products, score_samples(): jnp.einsum('icb,jcb->bij', block_codes, block_codes, precision=lax.Precis...  12.6 us
    reshape x2, local copies, waits for them, and re-layouts, score_samples(): flat = gram.reshape(count, table_count * table_count)  9.12 us
    select_n x2, other arithmetic, scorer(): picked_codes = jnp.take(got_codes[:, :, 0, :], positions, axis=0)  7.4 us
    all_to_all x1, starting transfers between devices, per_device(): lax.all_to_all(packed_scales.astype(jnp.bfloat16), 'tbl', split_axis=2, c...  7.31 us
    reshape x1, local copies, waits for them, and re-layouts, per_device(): codes.reshape(slot_count, column_count, tbl_count, batch_local)  7.22 us
    all_to_all x1, starting transfers between devices, per_device(): lax.all_to_all(packed_codes, 'tbl', split_axis=2, concat_axis=0, tiled=True)  6.03 us
  transfers between devices with their start and end apart: 2, of which 2 were waited for; matrix products, arithmetic and copies ran while one was open for 4% of the time, Pallas kernels for 0%

commit v1 on v0

v1 whole, which is shorter than its diff:
```python
import functools
import jax
import jax.numpy as jnp
import numpy as np
from jax import lax
from jax.sharding import PartitionSpec as P
from jax.experimental import pallas as pl
from jax.experimental.pallas import tpu as pltpu

LANES = 128


def pad_to(count, step):
    return -(-count // step) * step


def score_kernel(pos_ref, pool_ref, w1_ref, w2_ref, w3_ref, w4_ref, b1_ref, b2_ref, b3_ref, b4_ref, wo_ref, bo_ref,
                 out_ref, picked, wide, inter, w1, w2, w3, w4, pick_sem, weight_sem):
    shards, half, count = picked.shape
    tables = shards // 2
    weights = [
        pltpu.make_async_copy(src, dst, weight_sem.at[n])
        for n, (src, dst) in enumerate(((w1_ref, w1), (w2_ref, w2), (w3_ref, w3), (w4_ref, w4)))
    ]

    def fetch(shard):
        return pltpu.make_async_copy(pool_ref.at[pos_ref[shard]], picked.at[shard], pick_sem)

    def begin(shard, carry):
        fetch(shard).start()
        return carry

    def finish(shard, carry):
        fetch(shard).wait()
        return carry

    lax.fori_loop(0, shards, begin, 0)
    for copy in weights:
        copy.start()
    lax.fori_loop(0, shards, finish, 0)
    pairs = tables * (tables - 1) // 2
    rows = inter.shape[0]
    if rows > pairs:
        inter[pl.ds(pairs // 8 * 8, rows - pairs // 8 * 8), :] = jnp.zeros((rows - pairs // 8 * 8, count), jnp.float32)

    def gram_block(block, carry):
        lanes = pl.ds(pl.multiple_of(block * LANES, LANES), LANES)
        for shard in range(shards):
            wide[shard // 2, (shard % 2) * half:(shard % 2 + 1) * half, :] = picked[shard, :, lanes].astype(jnp.float32)
        row = 0
        for i in range(tables):
            left = wide[i]
            for j in range(i + 1, tables):
                inter[row:row + 1, lanes] = jnp.sum(left * wide[j], axis=0, keepdims=True)
                row += 1
        return carry

    lax.fori_loop(0, count // LANES, gram_block, 0)
    for copy in weights:
        copy.wait()
    step = 2 * LANES if count % (2 * LANES) == 0 else LANES

    def dense(hidden, weight, bias):
        product = jnp.dot(hidden, weight[...], preferred_element_type=jnp.float32)
        return jnp.maximum(product + bias[...], 0.0).astype(jnp.bfloat16)

    def top_block(block, carry):
        lanes = pl.ds(pl.multiple_of(block * step, step), step)
        hidden = jnp.transpose(inter[:, lanes]).astype(jnp.bfloat16)
        hidden = dense(hidden, w1, b1_ref)
        hidden = dense(hidden, w2, b2_ref)
        hidden = dense(hidden, w3, b3_ref)
        hidden = dense(hidden, w4, b4_ref)
        final = lax.dot_general(wo_ref[...], hidden, (((1,), (1,)), ((), ())), preferred_element_type=jnp.float32)
        out_ref[:, lanes] = final[0:1] + bo_ref[...]
        return carry

    lax.fori_loop(0, count // step, top_block, 0)


def score(pool, positions, layers):
    (w1, b1), (w2, b2), (w3, b3), (w4, b4), (wo, bo) = layers
    half, count = pool.shape[1:]
    shards = positions.shape[0]
    rows = pad_to(w1.shape[0], LANES)
    w1 = jnp.pad(w1, ((0, rows - w1.shape[0]), (0, 0)))
    wo = jnp.pad(wo[None, :], ((0, 7), (0, 0)))
    anywhere = pl.BlockSpec(memory_space=pl.ANY)
    vmem = pl.BlockSpec(memory_space=pltpu.VMEM)
    flops = 2 * count * sum(w.size for w in (w1, w2, w3, w4))
    return pl.pallas_call(
        score_kernel,
        out_shape=jax.ShapeDtypeStruct((1, count), jnp.float32),
        grid_spec=pltpu.PrefetchScalarGridSpec(
            num_scalar_prefetch=1,
            grid=(),
            in_specs=[anywhere] * 5 + [vmem] * 6,
            out_specs=vmem,
            scratch_shapes=[
                pltpu.VMEM((shards, half, count), pool.dtype),
                pltpu.VMEM((shards // 2, 2 * half, LANES), jnp.float32),
                pltpu.VMEM((rows, count), jnp.float32),
                pltpu.VMEM(w1.shape, w1.dtype),
                pltpu.VMEM(w2.shape, w2.dtype),
                pltpu.VMEM(w3.shape, w3.dtype),
                pltpu.VMEM(w4.shape, w4.dtype),
                pltpu.SemaphoreType.DMA,
                pltpu.SemaphoreType.DMA((4,)),
            ],
        ),
        compiler_params=pltpu.CompilerParams(vmem_limit_bytes=40 << 20),
        cost_estimate=pl.CostEstimate(flops=flops, bytes_accessed=shards * half * count * 2, transcendentals=0),
        name="score",
    )(positions, pool, w1, w2, w3, w4, b1[None, :], b2[None, :], b3[None, :], b4[None, :], wo, bo[None, :])


TABLES = 27


def shard_positions(slot_table, shard_total):
    flat = slot_table.reshape(-1)
    matches = flat[None, :] == jnp.arange(shard_total, dtype=jnp.int32)[:, None]
    places = jnp.arange(flat.shape[0], dtype=jnp.int32)[None, :]
    return jnp.sum(jnp.where(matches, places, 0), axis=1)


def per_device(codes, scales, shard_slot, *parameters):
    layers = tuple(zip(parameters[0::2], parameters[1::2]))
    slot_count, half, samples = codes.shape
    tbl_count = lax.axis_size("tbl")
    count = samples // tbl_count
    values = (codes.astype(jnp.float32) * scales[:, None, :]).astype(jnp.bfloat16)
    packed = values.reshape(slot_count, half, tbl_count, count).transpose(2, 0, 1, 3)
    received = lax.all_to_all(packed, "tbl", split_axis=0, concat_axis=0, tiled=True)
    pool = received.reshape(tbl_count * slot_count, half, count)
    positions = shard_positions(shard_slot, 2 * TABLES)
    logits = score(pool, positions, layers)
    return lax.all_gather(logits, "pair", axis=0, tiled=True)


def solution(mesh):
    return jax.shard_map(
        per_device,
        mesh=mesh,
        in_specs=(P("tbl", None, "pair"), P("tbl", "pair")) + (P(),) * 11,
        out_specs=P(None, "tbl"),
        check_vma=False,
    )
```

time: 244 us -> 198 us (0.81)
  local copies, waits for them, and re-layouts: 39.8 us -> 7.04 us
  matrix products: 17 us -> 0 us
  Pallas kernels: 0 us -> 13 us
  starting transfers between devices: 13.3 us -> 7.45 us
  other arithmetic: 8.71 us -> 5.2 us
    gather x6 -> x0, local copies, waits for them, and re-layouts: 21.7 us -> none  [the longest x2 18.8 us: scorer(): picked_codes = jnp.take(got_codes[:, :, 0, :], positions, axis=0)]
    dot_general x7 -> x0, matrix products: 17 us -> none  [the longest x2 12.6 us: score_samples(): jnp.einsum('icb,jcb->bij', block_codes, block_codes, precision=lax.Precis...]
    pallas_call x0 -> x1, Pallas kernels: none -> 13 us  [score(): pl.pallas_call(score_kernel, out_shape=jax.ShapeDtypeStruct((1, count), j...]
    reshape x3 -> x1, local copies, waits for them, and re-layouts: 16.3 us -> 3.91 us  [per_device(): values.reshape(slot_count, half, tbl_count, count).transpose(2, 0, 1, 3)]
    select_n x3 -> x0, other arithmetic: 7.44 us -> none  [the longest x2 7.4 us: scorer(): picked_codes = jnp.take(got_codes[:, :, 0, :], positions, axis=0)]
    all_to_all x2 -> x1, starting transfers between devices: 13.3 us -> 7.45 us  [per_device(): lax.all_to_all(packed, 'tbl', split_axis=0, concat_axis=0, tiled=True)]
    convert_element_type x2 -> x1, other arithmetic: 1.13 us -> 5.09 us  [per_device(): (codes.astype(jnp.float32) * scales[:, None, :]).astype(jnp.bfloat16)]
    all_to_all x2 -> x1, waiting for transfers between devices: 158 us -> 159 us  [per_device(): lax.all_to_all(packed, 'tbl', split_axis=0, concat_axis=0, tiled=True)]
  transfers between devices with their start and end apart: 2 -> 1, of which waited for: 2 -> 1; matrix products, arithmetic and copies ran while one was open for 4% -> 1% of each run, Pallas kernels for 0% -> 0%
where the time goes in v1:
time: 198 us; the launch traced here: 197 us
  waiting for transfers between devices  159 us (80%)
  Pallas kernels  13 us (7%)
  starting transfers between devices  7.45 us (4%)
  local copies, waits for them, and re-layouts  7.04 us (4%)
  other arithmetic  5.2 us (3%)
  blocking collectives  5.19 us (3%)
    all_to_all x1, waiting for transfers between devices, per_device(): lax.all_to_all(packed, 'tbl', split_axis=0, concat_axis=0, tiled=True)  159 us
    pallas_call x1, Pallas kernels, score(): pl.pallas_call(score_kernel, out_shape=jax.ShapeDtypeStruct((1, count), j...  13 us
    all_to_all x1, starting transfers between devices, per_device(): lax.all_to_all(packed, 'tbl', split_axis=0, concat_axis=0, tiled=True)  7.45 us
    all_gather x1, blocking collectives, per_device(): return lax.all_gather(logits, 'pair', axis=0, tiled=True)  5.19 us
    convert_element_type x1, other arithmetic, per_device(): (codes.astype(jnp.float32) * scales[:, None, :]).astype(jnp.bfloat16)  5.09 us
  transfers between devices with their start and end apart: 1, of which 1 were waited for; matrix products, arithmetic and copies ran while one was open for 1% of the time, Pallas kernels for 0%

profile of v1, /device:TPU:0, one launch (start us, length us, event | category | flops | bytes accessed | tf_op | source)
XLA Modules:
  0.0 197.3 jit_solution(381152871286220429)
XLA Ops:
  0.0 5.1 %multiply_convert_fusion = bf16[14,64,4096]{2,1,0:T(8,128)(2,1)S(1)} fusion(bf16[14,64,4096]{2,1,0:T(8,128)(2,1)} %param.13, f32[14,4096]{1,0:T(8,128)} %param.14), kind=kLoop, calls=%fused_computation | loop fusion | flops 11010048 | bytes 14909440 | tf_op jit(solution)/shard_map/convert_element_type | solution.py:132
  5.1 3.9 %copy.21 = bf16[14,8,8,8,512]{4,3,1,0,2:T(8,128)(2,1)} copy(bf16[14,8,8,8,512]{4,3,2,1,0:T(8,128)(2,1)S(1)} %bitcast.23) | data formatting | bytes 14680064 | tf_op jit(solution)/shard_map/reshape | solution.py:133
  9.0 0.0 copy-start.8
  9.0 0.0 copy-start.7
  9.0 0.0 copy-start
  9.0 0.0 copy-start.2
  9.0 0.0 copy-start.3
  9.0 0.0 copy-start.4
  9.0 0.0 copy-start.5
  9.1 0.0 copy-start.6
  9.1 7.5 %all-to-all-start = ((bf16[8,14,64,512]{3,2,1,0:T(8,128)(2,1)}), bf16[8,14,64,512]{3,2,1,0:T(8,128)(2,1)}, u32[]{:S(2)}, u32[]{:S(2)}) async-start(bf16[8,14,64,512]{3,2,1,0:T(8,128)(2,1)} %bitcast.24), calls=%async_computation | async-start | bytes 14680064 | tf_op jit(solution)/shard_map/all_to_all | solution.py:134
  16.5 0.0 copy-done.8
  16.5 1.2 pad.8.w1_ref
  17.7 0.0 copy-done.7
  17.7 0.1 eq.15
  18.5 0.1 select_reduce_fusion.pos_ref
  18.6 158.6 %all-to-all-done = bf16[8,14,64,512]{3,2,1,0:T(8,128)(2,1)} async-done(((bf16[8,14,64,512]{3,2,1,0:T(8,128)(2,1)}), bf16[8,14,64,512]{3,2,1,0:T(8,128)(2,1)}, u32[]{:S(2)}, u32[]{:S(2)}) %all-to-all-start) | async-done | bytes 7340064 | tf_op jit(solution)/shard_map/all_to_all | solution.py:134
  177.2 0.0 copy-done
  177.2 0.0 copy-done.2
  177.2 0.0 copy-done.3
  177.2 0.0 copy-done.4
  177.2 0.0 copy-done.5
  177.3 0.0 copy-done.6
  177.3 0.0 copy-start.1
  177.3 1.2 copy-done.1
  178.5 13.0 %score.1 = f32[1,512]{1,0:T(1,128)S(1)} custom-call(s32[54]{0:T(128)S(1)} %select_reduce_fusion.pos_ref, bf16[112,64,512]{2,1,0:T(8,128)(2,1)} %bitcast.1.pool_ref, bf16[384,1024]{1,0:T(8,128)(2,1)S(1)} %pad.8.w1_ref, bf16[1024,1024]{1,0:T(8,128)(2,1)S(1)} %copy-done, bf16[1024,512]{1,0:T(8,128)(2,1)S(1)} %copy-done.1, bf16[512,256]{1,0:T(8,128)(2,1)S(1)} %copy-done.2, ...), custom_call_target="tpu_custom_call" | custom-call | flops 2147483648 | bytes 3538944 | tf_op jit(solution)/shard_map/score/pallas_call | solution.py:91
  191.5 5.2 %all-gather = f32[4,1,512]{2,1,0:T(1,128)S(1)} all-gather(f32[1,1,512]{2,1,0:T(1,128)S(1)} %bitcast.18), channel_id=1, replica_groups=mesh['tbl'=8,'pair'=4] {'pair'}, dimensions={0}, use_global_device_ids=true | all-gather | bytes 10240 | tf_op jit(solution)/shard_map/all_gather | solution.py:138
  196.7 0.6 copy.22
  (2 shorter events, 0.0 us)
Async XLA Ops:
  9.0 7.5 %copy-start.8 = (bf16[256]{0:T(256)(128)(2,1)S(1)}, bf16[256]{0:T(256)(128)(2,1)}, u32[]{:S(2)}) copy-start(bf16[256]{0:T(256)(128)(2,1)} %param.24) | copy-start | bytes 1540
  9.0 8.7 %copy-start.7 = (s32[8,14]{1,0:T(8,128)S(1)}, s32[8,14]{1,0:T(8,128)}, u32[]{:S(2)}) copy-start(s32[8,14]{1,0:T(8,128)} %param.15) | copy-start | bytes 1348
  9.0 168.2 %copy-start = (bf16[1024,1024]{1,0:T(8,128)(2,1)S(1)}, bf16[1024,1024]{1,0:T(8,128)(2,1)}, u32[]{:S(2)}) copy-start(bf16[1024,1024]{1,0:T(8,128)(2,1)} %w2_ref.1) | copy-start | bytes 6291460
  9.0 168.2 %copy-start.2 = (bf16[512,256]{1,0:T(8,128)(2,1)S(1)}, bf16[512,256]{1,0:T(8,128)(2,1)}, u32[]{:S(2)}) copy-start(bf16[512,256]{1,0:T(8,128)(2,1)} %w4_ref.1) | copy-start | bytes 786436
  9.0 168.2 %copy-start.3 = (f32[1024]{0:T(1024)S(1)}, f32[1024]{0:T(1024)}, u32[]{:S(2)}) copy-start(f32[1024]{0:T(1024)} %param.17) | copy-start | bytes 12292
  9.0 168.2 %copy-start.4 = (f32[1024]{0:T(1024)S(1)}, f32[1024]{0:T(1024)}, u32[]{:S(2)}) copy-start(f32[1024]{0:T(1024)} %param.19) | copy-start | bytes 12292
  9.0 168.2 %copy-start.5 = (f32[512]{0:T(512)S(1)}, f32[512]{0:T(512)}, u32[]{:S(2)}) copy-start(f32[512]{0:T(512)} %param.21) | copy-start | bytes 6148
  9.1 168.2 %copy-start.6 = (f32[256]{0:T(256)S(1)}, f32[256]{0:T(256)}, u32[]{:S(2)}) copy-start(f32[256]{0:T(256)} %param.23) | copy-start | bytes 3076
  9.1 168.2 %all-to-all-start = ((bf16[8,14,64,512]{3,2,1,0:T(8,128)(2,1)}), bf16[8,14,64,512]{3,2,1,0:T(8,128)(2,1)}, u32[]{:S(2)}, u32[]{:S(2)}) async-start(bf16[8,14,64,512]{3,2,1,0:T(8,128)(2,1)} %bitcast.24), calls=%async_computation | async-start | bytes 14680064 | tf_op jit(solution)/shard_map/all_to_all | solution.py:134
  177.3 1.2 copy-start.1
